TPU v7x, 256 devices: a whole 4x4x8 slice. The times are simulated.
256 devices in a mesh: section: 8 (over z_lo, core), band: 32 (over x, z_hi, y).
Axes of the slice: x: 4, y: 4, z: 8 (z_hi: 2, z_lo: 4; z = z_hi * 4 + z_lo), core: 2. Of those that a mesh axis runs over, the one named last changes fastest.
Arguments:
- image: bfloat16 [64, 160, 320], P('band'), may hold values from -6 to 6
- carried: bfloat16 [8, 64, 160, 320], P('section', 'band'), may hold values from -6 to 6
- saved: bfloat16 [8, 64, 160, 320], P('section', 'band'), may hold values from -6 to 6
- sent_grad: bfloat16 [8, 64, 160, 320], P('section', 'band'), may hold values from -6 to 6
- loss_grad: bfloat16 [64, 160, 320], P('band'), may hold values from -6 to 6
- first_kernel: bfloat16 [8, 2880, 320], P('section'), may hold values from -0.109375 to 0.109375
- second_kernel: bfloat16 [8, 2880, 320], P('section'), may hold values from -0.109375 to 0.109375
Outputs:
- forward_out: bfloat16 [8, 64, 160, 320], P('section', 'band')
- input_grad: bfloat16 [8, 64, 160, 320], P('section', 'band')
- first_kernel_grad: float32 [8, 2880, 320], P('section', 'band')
- second_kernel_grad: float32 [8, 2880, 320], P('section', 'band')
All inputs are finite; a program needn't handle non-finite values.
Results may differ from a plain program's by a relative error of at most 0.0033.
Values may be sent and summed in bfloat16 or wider, within the bound.
A program may use at most 128 MiB of HBM per device.

v0:
```python
import functools
import math

import jax
import jax.numpy as jnp
from jax import lax
from jax.experimental import pallas as pl
from jax.experimental.pallas import tpu as pltpu
from jax.sharding import PartitionSpec as P

MESH = pl.DeviceIdType.MESH
BF16 = jnp.bfloat16
F32 = jnp.float32

H, W, C = 2, 160, 320
M = H * W
CL = 384
PIECE = 90
PR = 96
MAIN = 256
SEND = 5 * PR
NX, NY, NZ = 4, 4, 2


def dot(a, b):
    return jnp.dot(a, b, preferred_element_type=F32)


def dot_t(a, b):
    return lax.dot_general(a, b, (((1,), (1,)), ((), ())), preferred_element_type=F32)


def kernel(
    factor, image, carried, saved, sent_grad, loss_grad, first_hbm, second_hbm,
    fwd_hbm, igrad_hbm, gfirst_hbm, gsecond_hbm,
    first, second, xh, sh, gh, ah, ph, xs, ss, gs, as_, ps, shift_buf, slope, actt,
    terms, send1, recv1, held2, send2, recv2, send3, recv3, keep3, fwd, igrad, gout,
    load_sem, halo_send, halo_recv, s1_sem, r1_sem, s2_sem, r2_sem, s3_sem, r3_sem, out_sem,
):
    sec = lax.axis_index("section")
    band = lax.axis_index("band")
    nsec = lax.axis_size("section")
    nband = lax.axis_size("band")
    y = lax.rem(band, NY)
    z = lax.rem(lax.div(band, NY), NZ)
    x = lax.div(band, NY * NZ)
    next_sec = lax.rem(sec + 1, nsec)
    prev_sec = lax.rem(sec + nsec - 1, nsec)
    up = lax.rem(band + nband - 1, nband)
    down = lax.rem(band + 1, nband)

    def x_peer(d):
        return (sec, (lax.rem(x + d, NX) * NZ + z) * NY + y)

    def y_peer(d):
        return (sec, (x * NZ + z) * NY + lax.rem(y + d, NY))

    z_peer = (sec, (x * NZ + (1 - z)) * NY + y)

    loads = [
        pltpu.make_async_copy(saved, sh.at[pl.ds(1, H)], load_sem.at[0]),
        pltpu.make_async_copy(first_hbm, first, load_sem.at[1]),
        pltpu.make_async_copy(second_hbm, second, load_sem.at[2]),
    ]
    for copy in loads:
        copy.start()

    peers = [(next_sec, band), (next_sec, up), (next_sec, down)]
    peers += [(prev_sec, band), (prev_sec, up), (prev_sec, down)]
    peers += [(sec, up), (sec, down), z_peer]
    peers += [x_peer(d) for d in (1, 2, 3)] + [y_peer(d) for d in (1, 2, 3)]
    barrier = pltpu.get_barrier_semaphore()
    for peer in peers:
        pl.semaphore_signal(barrier, inc=1, device_id=peer, device_id_type=MESH)
    pl.semaphore_wait(barrier, len(peers))

    def remote(src, dst, send_sem, recv_sem, peer):
        return pltpu.make_async_remote_copy(
            src_ref=src, dst_ref=dst, send_sem=send_sem, recv_sem=recv_sem,
            device_id=peer, device_id_type=MESH,
        )

    def halos(src, held, to, k):
        return [
            remote(src.at[H - 1], held.at[0], halo_send.at[k], halo_recv.at[k], (to, down)),
            remote(src.at[0], held.at[H + 1], halo_send.at[k + 1], halo_recv.at[k + 1], (to, up)),
        ]

    def shifted_map(src, held, to, k):
        return halos(src, held, to, k) + [
            remote(src, held.at[pl.ds(1, H)], halo_send.at[k + 2], halo_recv.at[k + 2], (to, band))
        ]

    def start_all(copies):
        for copy in copies:
            copy.start()

    def wait_all(copies):
        for copy in copies:
            copy.wait()

    saved_halo = halos(saved, sh, sec, 0)
    start_all(saved_halo)

    g_copies = shifted_map(sent_grad, gh, prev_sec, 2)

    @pl.when(sec == 0)
    def _():
        start_all(shifted_map(loss_grad, gh, prev_sec, 2))

    @pl.when(sec != 0)
    def _():
        start_all(g_copies)

    x_copies = shifted_map(carried, xh, next_sec, 5)

    @pl.when(sec == nsec - 1)
    def _():
        start_all(shifted_map(image, xh, next_sec, 5))

    @pl.when(sec != nsec - 1)
    def _():
        start_all(x_copies)

    terms[pl.ds(9 * C, 8), :] = jnp.zeros((8, CL), F32)
    terms[:, pl.ds(MAIN, CL - MAIN)] = jnp.zeros((9 * C + 8, CL - MAIN), F32)
    shift_buf[pl.ds(0, 8), :] = jnp.zeros((8, C), F32)
    shift_buf[pl.ds(8 + 4 * W, 8), :] = jnp.zeros((8, C), F32)
    column = lax.broadcasted_iota(jnp.int32, (W, C), 0)

    def build(held, out):
        for r in range(H + 2):
            v = held[r]
            if r == 0:
                v = jnp.where(band == 0, jnp.zeros_like(v), v)
            if r == H + 1:
                v = jnp.where(band == nband - 1, jnp.zeros_like(v), v)
            out[1, pl.ds(r * W, W), :] = v
            shift_buf[pl.ds(8 + r * W, W), :] = v.astype(F32)
        for r in range(H + 2):
            low = shift_buf[pl.ds(7 + r * W, W), :]
            out[0, pl.ds(r * W, W), :] = jnp.where(column == 0, 0.0, low).astype(BF16)
            high = shift_buf[pl.ds(9 + r * W, W), :]
            out[2, pl.ds(r * W, W), :] = jnp.where(column == W - 1, 0.0, high).astype(BF16)

    def conv(maps, weights):
        total = None
        for tap in range(9):
            ky, kx = divmod(tap, 3)
            part = dot(maps[kx, pl.ds(ky * W, M), :], weights[pl.ds(tap * C, C), :])
            total = part if total is None else total + part
        return total

    def conv_t(maps, weights):
        total = None
        for tap in range(9):
            ky, kx = divmod(tap, 3)
            part = dot_t(maps[2 - kx, pl.ds((2 - ky) * W, M), :], weights[pl.ds(tap * C, C), :])
            total = part if total is None else total + part
        return total

    def wgrad(vt, maps):
        for tap in range(9):
            ky, kx = divmod(tap, 3)
            terms[pl.ds(tap * C, C), pl.ds(0, C)] = dot(
                vt[...], maps[2 - kx, pl.ds((2 - ky) * W, M), :]
            )

    lane = lax.broadcasted_iota(jnp.int32, (PR, 128), 1)

    def pack(k):
        for half in range(2):
            for dest in range(4):
                rests = []
                for j in range(4):
                    xx, yy = (dest, j) if half == 0 else (j, dest)
                    row = ((xx * NZ + half) * NY + yy) * PIECE
                    send1[k, half, dest, pl.ds(j * PR, PR), :] = terms[
                        pl.ds(row, PR), pl.ds(0, MAIN)
                    ].astype(BF16)
                    rests.append(terms[pl.ds(row, PR), pl.ds(MAIN, 128)])
                for j in range(2):
                    pair = jnp.where(
                        lane < 64, rests[2 * j], pltpu.roll(rests[2 * j + 1], 64, 1)
                    )
                    send1[k, half, dest, pl.ds(4 * PR, PR), pl.ds(j * 128, 128)] = pair.astype(BF16)

    def stage1(k):
        copies = []
        for d in (1, 3, 2):
            for half, (pos, peer) in enumerate(((x, x_peer), (y, y_peer))):
                copies.append(
                    remote(
                        send1.at[k, half, lax.rem(pos + d, 4)], recv1.at[k, half, d - 1],
                        s1_sem.at[k, half, d - 1], r1_sem.at[k, half, d - 1], peer(d),
                    )
                )
        return copies

    def stage2(k):
        copies = []
        for d in (1, 3, 2):
            for half, (pos, peer) in enumerate(((y, y_peer), (x, x_peer))):
                copies.append(
                    remote(
                        send2.at[k, half, lax.rem(pos + d, 4)], recv2.at[k, half, d - 1],
                        s2_sem.at[k, half, d - 1], r2_sem.at[k, half, d - 1], peer(d),
                    )
                )
        return copies

    def sum1(k):
        for half, pos in enumerate((x, y)):
            def total(rows, lanes):
                value = send1[k, half, pos, rows, lanes].astype(F32)
                for d in range(3):
                    value = value + recv1[k, half, d, rows, lanes].astype(F32)
                return value

            for j in range(4):
                main = total(pl.ds(j * PR, PR), pl.ds(0, MAIN))
                held2[k, half, j, :, pl.ds(0, MAIN)] = main
                send2[k, half, j, :, pl.ds(0, MAIN)] = main.astype(BF16)
            for j in range(2):
                rest = total(pl.ds(4 * PR, PR), pl.ds(j * 128, 128))
                for i, part in enumerate((rest, pltpu.roll(rest, 64, 1))):
                    held2[k, half, 2 * j + i, :, pl.ds(MAIN, 128)] = part
                    send2[k, half, 2 * j + i, :, pl.ds(MAIN, 128)] = part.astype(BF16)

    def sum2(k):
        sums = []
        for half, pos in enumerate((y, x)):
            value = held2[k, half, pos]
            for d in range(3):
                value = value + recv2[k, half, d].astype(F32)
            sums.append(value)
        keep3[k] = jnp.where(z == 0, sums[0], sums[1])
        send3[k] = jnp.where(z == 0, sums[1], sums[0]).astype(BF16)

    def stage3(k):
        return remote(send3.at[k], recv3.at[k], s3_sem.at[k], r3_sem.at[k], z_peer)

    loads[0].wait()
    wait_all(saved_halo)
    build(sh, ss)
    loads[1].wait()
    pre = conv(ss, first)
    sig = jax.nn.sigmoid(pre)
    actt[...] = jnp.transpose(pre * sig).astype(BF16)
    slope[...] = sig * (1.0 + pre * (1.0 - sig))
    wait_all(g_copies)
    build(gh, gs)
    wgrad(actt, gs)
    pack(1)
    second_1 = stage1(1)
    start_all(second_1)

    loads[2].wait()
    grad_pre = (conv_t(gs, second) * slope[...]).astype(BF16)
    for r in range(H):
        ph[1 + r] = grad_pre[r * W : (r + 1) * W]
    pre_halo = halos(ph.at[pl.ds(1, H)], ph, sec, 8)
    start_all(pre_halo)

    wait_all(x_copies)
    build(xh, xs)
    pre = conv(xs, first)
    act = (pre * jax.nn.sigmoid(pre)).astype(BF16)
    for r in range(H):
        ah[1 + r] = act[r * W : (r + 1) * W]
    act_halo = halos(ah.at[pl.ds(1, H)], ah, sec, 10)
    start_all(act_halo)

    wait_all(pre_halo)
    build(ph, ps)
    actt[...] = jnp.transpose(ss[1, pl.ds(W, M), :].astype(F32)).astype(BF16)
    wgrad(actt, ps)
    pack(0)
    first_1 = stage1(0)
    start_all(first_1)

    igrad_flat = conv_t(ps, first)
    for r in range(H):
        igrad[r] = (gh[1 + r].astype(F32) + igrad_flat[r * W : (r + 1) * W]).astype(BF16)
    outs = [pltpu.make_async_copy(igrad, igrad_hbm, out_sem.at[0])]
    outs[0].start()

    wait_all(second_1)
    sum1(1)
    second_2 = stage2(1)
    start_all(second_2)

    wait_all(act_halo)
    build(ah, as_)
    out_flat = conv(as_, second)
    for r in range(H):
        fwd[r] = (xh[1 + r].astype(F32) + out_flat[r * W : (r + 1) * W]).astype(BF16)
    outs.append(pltpu.make_async_copy(fwd, fwd_hbm, out_sem.at[1]))
    outs[1].start()

    wait_all(second_2)
    sum2(1)
    second_3 = stage3(1)
    second_3.start()

    wait_all(first_1)
    sum1(0)
    first_2 = stage2(0)
    start_all(first_2)

    second_3.wait()
    gout[1] = (keep3[1] + recv3[1].astype(F32))[:PIECE, :C] * factor
    outs.append(pltpu.make_async_copy(gout.at[1], gsecond_hbm, out_sem.at[2]))
    outs[2].start()

    wait_all(first_2)
    sum2(0)
    first_3 = stage3(0)
    first_3.start()
    first_3.wait()
    gout[0] = (keep3[0] + recv3[0].astype(F32))[:PIECE, :C] * factor
    outs.append(pltpu.make_async_copy(gout.at[0], gfirst_hbm, out_sem.at[3]))
    outs[3].start()
    for copy in outs:
        copy.wait()


def body(image, carried, saved, sent_grad, loss_grad, first_kernel, second_kernel):
    factor = 1.0 / math.sqrt(H * lax.axis_size("band") * W)
    any_spec = pl.BlockSpec(memory_space=pl.ANY)
    vmem, dma = pltpu.VMEM, pltpu.SemaphoreType.DMA
    halo_map = vmem((H + 2, W, C), BF16)
    moved = vmem((3, (H + 2) * W, C), BF16)
    fwd, igrad, gfirst, gsecond = pl.pallas_call(
        functools.partial(kernel, factor),
        out_shape=(
            jax.ShapeDtypeStruct((H, W, C), BF16),
            jax.ShapeDtypeStruct((H, W, C), BF16),
            jax.ShapeDtypeStruct((PIECE, C), F32),
            jax.ShapeDtypeStruct((PIECE, C), F32),
        ),
        in_specs=[any_spec] * 7,
        out_specs=(any_spec,) * 4,
        scratch_shapes=[
            vmem((9 * C, C), BF16), vmem((9 * C, C), BF16),
            halo_map, halo_map, halo_map, halo_map, halo_map,
            moved, moved, moved, moved, moved,
            vmem((16 + (H + 2) * W, C), F32),
            vmem((M, C), F32),
            vmem((C, M), BF16),
            vmem((9 * C + 8, CL), F32),
            vmem((2, 2, 4, SEND, MAIN), BF16), vmem((2, 2, 3, SEND, MAIN), BF16),
            vmem((2, 2, 4, PR, CL), F32), vmem((2, 2, 4, PR, CL), BF16),
            vmem((2, 2, 3, PR, CL), BF16),
            vmem((2, PR, CL), BF16), vmem((2, PR, CL), BF16), vmem((2, PR, CL), F32),
            vmem((H, W, C), BF16), vmem((H, W, C), BF16),
            vmem((2, PIECE, C), F32),
            dma((3,)), dma((12,)), dma((12,)),
            dma((2, 2, 3)), dma((2, 2, 3)), dma((2, 2, 3)), dma((2, 2, 3)),
            dma((2,)), dma((2,)), dma((4,)),
        ],
        compiler_params=pltpu.CompilerParams(
            collective_id=0, has_side_effects=True, vmem_limit_bytes=56 * 1024 * 1024
        ),
    )(image, carried[0], saved[0], sent_grad[0], loss_grad, first_kernel[0], second_kernel[0])
    return fwd[None], igrad[None], gfirst[None], gsecond[None]


def solution(mesh):
    return jax.shard_map(
        body,
        mesh=mesh,
        in_specs=(
            P("band", None, None),
            P("section", "band", None, None),
            P("section", "band", None, None),
            P("section", "band", None, None),
            P("band", None, None),
            P("section", None, None),
            P("section", None, None),
        ),
        out_specs=(
            P("section", "band", None, None),
            P("section", "band", None, None),
            P("section", "band", None),
            P("section", "band", None),
        ),
        check_vma=False,
    )
```

profile of v0, /device:TPU:1, one launch (start us, length us, event | category | flops | bytes accessed | tf_op | source)
XLA Modules:
  0.0 93.9 jit_solution(9824833375446980602)
XLA Ops:
  0.6 0.0 copy-start
  0.6 4.1 %copy.11 = bf16[1,2880,320]{2,1,0:T(8,128)(2,1)} copy(bf16[1,2880,320]{1,2,0:T(8,128)(2,1)} %param.12) | data formatting | bytes 3686400 | tf_op args[5]
  4.8 0.0 copy-done
  4.8 2.6 %copy.12 = bf16[1,2880,320]{2,1,0:T(8,128)(2,1)} copy(bf16[1,2880,320]{1,2,0:T(8,128)(2,1)S(1)} %copy-done) | data formatting | bytes 3686400 | tf_op args[6]
  7.4 79.8 %shard_map.102 = (bf16[2,160,320]{2,1,0:T(8,128)(2,1)}, bf16[2,160,320]{2,1,0:T(8,128)(2,1)}, f32[90,320]{1,0:T(8,128)}, f32[90,320]{1,0:T(8,128)}) custom-call(bf16[2,160,320]{2,1,0:T(8,128)(2,1)} %image.1, bf16[2,160,320]{2,1,0:T(8,128)(2,1)} %bitcast.11, bf16[2,160,320]{2,1,0:T(8,128)(2,1)} %bitcast.12, bf16[2,160,320]{2,1,0:T(8,128)(2,1)} %bitcast.13, ...), custom_call_target="tpu_custom_call" | custom-call | tf_op jit(solution)/shard_map/pallas_call | solution.py:334
  87.1 1.7 %copy.13 = f32[1,90,320]{2,0,1:T(1,128)} copy(f32[1,90,320]{2,1,0:T(8,128)} %bitcast.17) | data formatting | bytes 230400
  88.8 1.7 %copy.14 = f32[1,90,320]{2,0,1:T(1,128)} copy(f32[1,90,320]{2,1,0:T(8,128)} %bitcast.16) | data formatting | bytes 230400
  90.6 1.7 %copy.17 = bf16[1,2,160,320]{3,2,1,0:T(8,128)(2,1)} copy(bf16[1,2,160,320]{3,2,1,0:T(8,128)(2,1)} %bitcast.15) | data formatting | bytes 409600
  92.2 1.7 %copy.18 = bf16[1,2,160,320]{3,2,1,0:T(8,128)(2,1)} copy(bf16[1,2,160,320]{3,2,1,0:T(8,128)(2,1)} %bitcast.14) | data formatting | bytes 409600
Async XLA Ops:
  0.6 4.1 %copy-start = (bf16[1,2880,320]{1,2,0:T(8,128)(2,1)S(1)}, bf16[1,2880,320]{1,2,0:T(8,128)(2,1)}, u32[]{:S(2)}) copy-start(bf16[1,2880,320]{1,2,0:T(8,128)(2,1)} %param.13) | copy-start | bytes 5529604
where the time goes:
time: 94.1 us; the launch traced here: 93.9 us
  Pallas kernels  79.8 us (85%)
  local copies, waits for them, and re-layouts  13.5 us (14%)
    pallas_call x1, Pallas kernels, body(): pl.pallas_call(functools.partial(kernel, factor), out_shape=(jax.ShapeDty...  79.8 us
    unnamed x8, local copies, waits for them, and re-layouts  13.5 us

commit v1 on v0

--- a/solution.py
+++ b/solution.py
@@ -33,8 +33,8 @@
 def kernel(
     factor, image, carried, saved, sent_grad, loss_grad, first_hbm, second_hbm,
     fwd_hbm, igrad_hbm, gfirst_hbm, gsecond_hbm,
-    first, second, xh, sh, gh, ah, ph, xs, ss, gs, as_, ps, shift_buf, slope, actt,
-    terms, send1, recv1, held2, send2, recv2, send3, recv3, keep3, fwd, igrad, gout,
+    first_t, second_t, first, second, xh, sh, gh, ah, ph, xs, ss, gs, as_, ps, shift_buf, slope, actt,
+    terms, send1, relay, recv1, held2, send2, recv2, send3, recv3, keep3, fwd, igrad, gout,
     load_sem, halo_send, halo_recv, s1_sem, r1_sem, s2_sem, r2_sem, s3_sem, r3_sem, out_sem,
 ):
     sec = lax.axis_index("section")
@@ -59,11 +59,13 @@
 
     loads = [
         pltpu.make_async_copy(saved, sh.at[pl.ds(1, H)], load_sem.at[0]),
-        pltpu.make_async_copy(first_hbm, first, load_sem.at[1]),
-        pltpu.make_async_copy(second_hbm, second, load_sem.at[2]),
+        pltpu.make_async_copy(first_hbm, first_t, load_sem.at[1]),
+        pltpu.make_async_copy(second_hbm, second_t, load_sem.at[2]),
     ]
     for copy in loads:
         copy.start()
+    local_g = pltpu.make_async_copy(loss_grad, gh.at[pl.ds(1, H)], load_sem.at[3])
+    local_x = pltpu.make_async_copy(image, xh.at[pl.ds(1, H)], load_sem.at[4])
 
     peers = [(next_sec, band), (next_sec, up), (next_sec, down)]
     peers += [(prev_sec, band), (prev_sec, up), (prev_sec, down)]
@@ -72,6 +74,17 @@
     barrier = pltpu.get_barrier_semaphore()
     for peer in peers:
         pl.semaphore_signal(barrier, inc=1, device_id=peer, device_id_type=MESH)
+
+    def turn(source, target):
+        for k in range(0, 9 * C, 640):
+            n = min(640, 9 * C - k)
+            target[pl.ds(k, n), :] = jnp.transpose(source[:, pl.ds(k, n)])
+
+    loads[1].wait()
+    turn(first_t, first)
+    loads[2].wait()
+    turn(second_t, second)
+
     pl.semaphore_wait(barrier, len(peers))
 
     def remote(src, dst, send_sem, recv_sem, peer):
@@ -102,25 +115,40 @@
     saved_halo = halos(saved, sh, sec, 0)
     start_all(saved_halo)
 
-    g_copies = shifted_map(sent_grad, gh, prev_sec, 2)
-
-    @pl.when(sec == 0)
-    def _():
-        start_all(shifted_map(loss_grad, gh, prev_sec, 2))
-
-    @pl.when(sec != 0)
-    def _():
-        start_all(g_copies)
-
-    x_copies = shifted_map(carried, xh, next_sec, 5)
-
-    @pl.when(sec == nsec - 1)
-    def _():
-        start_all(shifted_map(image, xh, next_sec, 5))
-
-    @pl.when(sec != nsec - 1)
-    def _():
-        start_all(x_copies)
+    def start_map(src, edge_src, local, held, to, k, edge):
+        @pl.when(sec == edge)
+        def _():
+            start_all(halos(edge_src, held, sec, k + 3))
+            local.start()
+
+        @pl.when(sec != nsec - 1 - edge)
+        def _():
+            start_all(shifted_map(src, held, to, k))
+
+    def wait_map(src, edge_src, local, held, to, k, edge):
+        copies = shifted_map(src, held, to, k)
+
+        @pl.when(sec != nsec - 1 - edge)
+        def _():
+            for copy in copies:
+                copy.wait_send()
+
+        @pl.when(sec == edge)
+        def _():
+            edges = halos(edge_src, held, sec, k + 3)
+            for copy in edges:
+                copy.wait_send()
+                copy.wait_recv()
+            local.wait()
+
+        @pl.when(sec != edge)
+        def _():
+            for copy in copies:
+                copy.wait_recv()
+
+    g_map = (sent_grad, loss_grad, local_g, gh, prev_sec, 2, nsec - 1)
+    x_map = (carried, image, local_x, xh, next_sec, 7, 0)
+    start_map(*g_map)
 
     terms[pl.ds(9 * C, 8), :] = jnp.zeros((8, CL), F32)
     terms[:, pl.ds(MAIN, CL - MAIN)] = jnp.zeros((9 * C + 8, CL - MAIN), F32)
@@ -185,17 +213,30 @@
                     )
                     send1[k, half, dest, pl.ds(4 * PR, PR), pl.ds(j * 128, 128)] = pair.astype(BF16)
 
+    low, high = pl.ds(0, SEND // 2), pl.ds(SEND // 2, SEND // 2)
+
     def stage1(k):
-        copies = []
-        for d in (1, 3, 2):
-            for half, (pos, peer) in enumerate(((x, x_peer), (y, y_peer))):
-                copies.append(
-                    remote(
-                        send1.at[k, half, lax.rem(pos + d, 4)], recv1.at[k, half, d - 1],
-                        s1_sem.at[k, half, d - 1], r1_sem.at[k, half, d - 1], peer(d),
+        relays, plain, added = [], [], []
+        for half, (pos, peer) in enumerate(((x, x_peer), (y, y_peer))):
+            for side, (d, via, own) in enumerate(((1, low, high), (3, high, low))):
+                def copy(ahead, rows, dst, i):
+                    return remote(
+                        send1.at[k, half, lax.rem(pos + ahead, 4), rows], dst,
+                        s1_sem.at[k, half, i + side], r1_sem.at[k, half, i + side], peer(d),
                     )
-                )
-        return copies
+
+                relays.append(copy(2, via, relay.at[k, half, side], 0))
+                plain.append(copy(d, own, recv1.at[k, half, side, own], 2))
+                added.append(copy(d, via, recv1.at[k, half, side, via], 4))
+        return relays, plain, added
+
+    def add_relays(k):
+        for half, pos in enumerate((x, y)):
+            for side, (d, via) in enumerate(((1, low), (3, high))):
+                ahead = lax.rem(pos + d, 4)
+                send1[k, half, ahead, via, :] = (
+                    send1[k, half, ahead, via, :].astype(F32) + relay[k, half, side].astype(F32)
+                ).astype(BF16)
 
     def stage2(k):
         copies = []
@@ -213,7 +254,7 @@
         for half, pos in enumerate((x, y)):
             def total(rows, lanes):
                 value = send1[k, half, pos, rows, lanes].astype(F32)
-                for d in range(3):
+                for d in range(2):
                     value = value + recv1[k, half, d, rows, lanes].astype(F32)
                 return value
 
@@ -243,52 +284,76 @@
     loads[0].wait()
     wait_all(saved_halo)
     build(sh, ss)
-    loads[1].wait()
     pre = conv(ss, first)
     sig = jax.nn.sigmoid(pre)
     actt[...] = jnp.transpose(pre * sig).astype(BF16)
     slope[...] = sig * (1.0 + pre * (1.0 - sig))
-    wait_all(g_copies)
+    wait_map(*g_map)
+    start_map(*x_map)
     build(gh, gs)
     wgrad(actt, gs)
     pack(1)
-    second_1 = stage1(1)
-    start_all(second_1)
-
-    loads[2].wait()
+    second_relays, second_plain, second_added = stage1(1)
+    start_all(second_relays + second_plain)
+
     grad_pre = (conv_t(gs, second) * slope[...]).astype(BF16)
     for r in range(H):
         ph[1 + r] = grad_pre[r * W : (r + 1) * W]
-    pre_halo = halos(ph.at[pl.ds(1, H)], ph, sec, 8)
+    pre_halo = halos(ph.at[pl.ds(1, H)], ph, sec, 12)
     start_all(pre_halo)
 
-    wait_all(x_copies)
+    for tap in range(9):
+        ky, kx = divmod(tap, 3)
+        terms[pl.ds(tap * C, C), pl.ds(0, C)] = dot(
+            jnp.transpose(ss[kx, pl.ds(ky * W, M), :]), grad_pre
+        )
+    wait_all(second_relays)
+    add_relays(1)
+    start_all(second_added)
+    pack(0)
+    first_relays, first_plain, first_added = stage1(0)
+    start_all(first_relays + first_plain)
+
+    wait_map(*x_map)
     build(xh, xs)
     pre = conv(xs, first)
     act = (pre * jax.nn.sigmoid(pre)).astype(BF16)
     for r in range(H):
         ah[1 + r] = act[r * W : (r + 1) * W]
-    act_halo = halos(ah.at[pl.ds(1, H)], ah, sec, 10)
+    act_halo = halos(ah.at[pl.ds(1, H)], ah, sec, 14)
     start_all(act_halo)
+
+    wait_all(first_relays)
+    add_relays(0)
+    start_all(first_added)
+
+    wait_all(second_plain + second_added)
+    sum1(1)
+    second_2 = stage2(1)
+    start_all(second_2)
 
     wait_all(pre_halo)
     build(ph, ps)
-    actt[...] = jnp.transpose(ss[1, pl.ds(W, M), :].astype(F32)).astype(BF16)
-    wgrad(actt, ps)
-    pack(0)
-    first_1 = stage1(0)
-    start_all(first_1)
-
     igrad_flat = conv_t(ps, first)
     for r in range(H):
         igrad[r] = (gh[1 + r].astype(F32) + igrad_flat[r * W : (r + 1) * W]).astype(BF16)
     outs = [pltpu.make_async_copy(igrad, igrad_hbm, out_sem.at[0])]
     outs[0].start()
 
-    wait_all(second_1)
-    sum1(1)
-    second_2 = stage2(1)
-    start_all(second_2)
+    wait_all(first_plain + first_added)
+    sum1(0)
+    first_2 = stage2(0)
+    start_all(first_2)
+
+    wait_all(second_2)
+    sum2(1)
+    second_3 = stage3(1)
+    second_3.start()
+
+    wait_all(first_2)
+    sum2(0)
+    first_3 = stage3(0)
+    first_3.start()
 
     wait_all(act_halo)
     build(ah, as_)
@@ -298,31 +363,20 @@
     outs.append(pltpu.make_async_copy(fwd, fwd_hbm, out_sem.at[1]))
     outs[1].start()
 
-    wait_all(second_2)
-    sum2(1)
-    second_3 = stage3(1)
-    second_3.start()
-
-    wait_all(first_1)
-    sum1(0)
-    first_2 = stage2(0)
-    start_all(first_2)
-
-    second_3.wait()
-    gout[1] = (keep3[1] + recv3[1].astype(F32))[:PIECE, :C] * factor
-    outs.append(pltpu.make_async_copy(gout.at[1], gsecond_hbm, out_sem.at[2]))
-    outs[2].start()
-
-    wait_all(first_2)
-    sum2(0)
-    first_3 = stage3(0)
-    first_3.start()
-    first_3.wait()
-    gout[0] = (keep3[0] + recv3[0].astype(F32))[:PIECE, :C] * factor
-    outs.append(pltpu.make_async_copy(gout.at[0], gfirst_hbm, out_sem.at[3]))
-    outs[3].start()
+    for k, copy, out in ((1, second_3, gsecond_hbm), (0, first_3, gfirst_hbm)):
+        copy.wait()
+        gout[k] = (keep3[k] + recv3[k].astype(F32))[:PIECE, :C] * factor
+        outs.append(pltpu.make_async_copy(gout.at[k], out, out_sem.at[3 - k]))
+        outs[-1].start()
     for copy in outs:
         copy.wait()
+
+
+def copy_out(fwd, igrad, gfirst, gsecond, fwd_out, igrad_out, gfirst_out, gsecond_out):
+    fwd_out[...] = fwd[...]
+    igrad_out[...] = igrad[...]
+    gfirst_out[...] = gfirst[...].reshape(PIECE, 1, C)
+    gsecond_out[...] = gsecond[...].reshape(PIECE, 1, C)
 
 
 def body(image, carried, saved, sent_grad, loss_grad, first_kernel, second_kernel):
@@ -342,6 +396,7 @@
         in_specs=[any_spec] * 7,
         out_specs=(any_spec,) * 4,
         scratch_shapes=[
+            vmem((C, 9 * C), BF16), vmem((C, 9 * C), BF16),
             vmem((9 * C, C), BF16), vmem((9 * C, C), BF16),
             halo_map, halo_map, halo_map, halo_map, halo_map,
             moved, moved, moved, moved, moved,
@@ -349,21 +404,30 @@
             vmem((M, C), F32),
             vmem((C, M), BF16),
             vmem((9 * C + 8, CL), F32),
-            vmem((2, 2, 4, SEND, MAIN), BF16), vmem((2, 2, 3, SEND, MAIN), BF16),
+            vmem((2, 2, 4, SEND, MAIN), BF16), vmem((2, 2, 2, SEND // 2, MAIN), BF16),
+            vmem((2, 2, 2, SEND, MAIN), BF16),
             vmem((2, 2, 4, PR, CL), F32), vmem((2, 2, 4, PR, CL), BF16),
             vmem((2, 2, 3, PR, CL), BF16),
             vmem((2, PR, CL), BF16), vmem((2, PR, CL), BF16), vmem((2, PR, CL), F32),
             vmem((H, W, C), BF16), vmem((H, W, C), BF16),
             vmem((2, PIECE, C), F32),
-            dma((3,)), dma((12,)), dma((12,)),
-            dma((2, 2, 3)), dma((2, 2, 3)), dma((2, 2, 3)), dma((2, 2, 3)),
+            dma((5,)), dma((16,)), dma((16,)),
+            dma((2, 2, 6)), dma((2, 2, 6)), dma((2, 2, 3)), dma((2, 2, 3)),
             dma((2,)), dma((2,)), dma((4,)),
         ],
         compiler_params=pltpu.CompilerParams(
             collective_id=0, has_side_effects=True, vmem_limit_bytes=56 * 1024 * 1024
         ),
-    )(image, carried[0], saved[0], sent_grad[0], loss_grad, first_kernel[0], second_kernel[0])
-    return fwd[None], igrad[None], gfirst[None], gsecond[None]
+    )(image, carried[0], saved[0], sent_grad[0], loss_grad, first_kernel[0].T, second_kernel[0].T)
+    vmem_spec = pl.BlockSpec(memory_space=pltpu.VMEM)
+    grad_shape = jax.ShapeDtypeStruct((PIECE, 1, C), F32)
+    fwd, igrad, gfirst, gsecond = pl.pallas_call(
+        copy_out,
+        out_shape=(fwd, igrad, grad_shape, grad_shape),
+        in_specs=[vmem_spec] * 4,
+        out_specs=(vmem_spec,) * 4,
+    )(fwd, igrad, gfirst, gsecond)
+    return fwd[None], igrad[None], gfirst.reshape(1, PIECE, C), gsecond.reshape(1, PIECE, C)
 
 
 def solution(mesh):

time: 94.1 us -> 72.3 us (0.77)
  the two profiles are of different devices: /device:TPU:1 before, /device:TPU:6 now
where the time goes in v1:
time: 72.3 us; the launch traced here: 72.2 us
  Pallas kernels  71.5 us (99%)
    pallas_call x1, Pallas kernels, body(): pl.pallas_call(functools.partial(kernel, factor), out_shape=(jax.ShapeDty...  69.4 us
    pallas_call x1, Pallas kernels, body(): pl.pallas_call(copy_out, out_shape=(fwd, igrad, grad_shape, grad_shape),...  2.12 us

profile of v1, /device:TPU:6, one launch (start us, length us, event | category | flops | bytes accessed | tf_op | source)
XLA Modules:
  0.0 72.2 jit_solution(3012735817034208324)
XLA Ops:
  0.6 69.4 %shard_map.102 = (bf16[2,160,320]{2,1,0:T(8,128)(2,1)}, bf16[2,160,320]{2,1,0:T(8,128)(2,1)}, f32[90,320]{1,0:T(8,128)}, f32[90,320]{1,0:T(8,128)}) custom-call(bf16[2,160,320]{2,1,0:T(8,128)(2,1)} %image.1, bf16[2,160,320]{2,1,0:T(8,128)(2,1)} %bitcast.15, bf16[2,160,320]{2,1,0:T(8,128)(2,1)} %bitcast.16, bf16[2,160,320]{2,1,0:T(8,128)(2,1)} %bitcast.17, ...), custom_call_target="tpu_custom_call" | custom-call | tf_op jit(solution)/shard_map/pallas_call | solution.py:388
  70.1 2.1 %shard_map.103 = (bf16[2,160,320]{2,1,0:T(8,128)(2,1)}, bf16[2,160,320]{2,1,0:T(8,128)(2,1)}, f32[90,1,320]{2,1,0:T(1,128)}, f32[90,1,320]{2,1,0:T(1,128)}) custom-call(bf16[2,160,320]{2,1,0:T(8,128)(2,1)} %get-tuple-element.12.fwd, bf16[2,160,320]{2,1,0:T(8,128)(2,1)} %get-tuple-element.13.igrad, f32[90,320]{1,0:T(8,128)} %get-tuple-element.14.gfirst, ...), custom_call_target="tpu_custom_call" | custom-call | tf_op jit(solution)/shard_map/pallas_call | solution.py:424

commit v2 on v1

--- a/solution.py
+++ b/solution.py
@@ -19,6 +19,8 @@
 PR = 96
 MAIN = 256
 SEND = 5 * PR
+Q = W // 4
+ROW = W + Q
 NX, NY, NZ = 4, 4, 2
 
 
@@ -33,7 +35,7 @@
 def kernel(
     factor, image, carried, saved, sent_grad, loss_grad, first_hbm, second_hbm,
     fwd_hbm, igrad_hbm, gfirst_hbm, gsecond_hbm,
-    first_t, second_t, first, second, xh, sh, gh, ah, ph, xs, ss, gs, as_, ps, shift_buf, slope, actt,
+    first_t, second_t, first, second, raw, gsend, xsend, xh, sh, gh, ah, ph, xs, ss, gs, as_, ps, shift_buf, slope, actt,
     terms, send1, relay, recv1, held2, send2, recv2, send3, recv3, keep3, fwd, igrad, gout,
     load_sem, halo_send, halo_recv, s1_sem, r1_sem, s2_sem, r2_sem, s3_sem, r3_sem, out_sem,
 ):
@@ -58,14 +60,15 @@
     z_peer = (sec, (x * NZ + (1 - z)) * NY + y)
 
     loads = [
-        pltpu.make_async_copy(saved, sh.at[pl.ds(1, H)], load_sem.at[0]),
-        pltpu.make_async_copy(first_hbm, first_t, load_sem.at[1]),
-        pltpu.make_async_copy(second_hbm, second_t, load_sem.at[2]),
+        pltpu.make_async_copy(value, raw.at[i], load_sem.at[i])
+        for i, value in enumerate((saved, sent_grad, carried, loss_grad, image))
+    ]
+    loads += [
+        pltpu.make_async_copy(first_hbm, first_t, load_sem.at[5]),
+        pltpu.make_async_copy(second_hbm, second_t, load_sem.at[6]),
     ]
     for copy in loads:
         copy.start()
-    local_g = pltpu.make_async_copy(loss_grad, gh.at[pl.ds(1, H)], load_sem.at[3])
-    local_x = pltpu.make_async_copy(image, xh.at[pl.ds(1, H)], load_sem.at[4])
 
     peers = [(next_sec, band), (next_sec, up), (next_sec, down)]
     peers += [(prev_sec, band), (prev_sec, up), (prev_sec, down)]
@@ -75,15 +78,31 @@
     for peer in peers:
         pl.semaphore_signal(barrier, inc=1, device_id=peer, device_id_type=MESH)
 
-    def turn(source, target):
-        for k in range(0, 9 * C, 640):
-            n = min(640, 9 * C - k)
-            target[pl.ds(k, n), :] = jnp.transpose(source[:, pl.ds(k, n)])
-
+    def pack_map(i, target, start):
+        for r in range(H):
+            target[start + r, pl.ds(0, W), :] = raw[i, r, :, pl.ds(0, MAIN)]
+            rest = raw[i, r, :, pl.ds(MAIN, C - MAIN)].astype(F32)
+            for j in range(2):
+                one, two = rest[2 * j * Q : (2 * j + 1) * Q], rest[(2 * j + 1) * Q : (2 * j + 2) * Q]
+                pair = jnp.concatenate([one, two], axis=1)
+                target[start + r, pl.ds(W, Q), pl.ds(128 * j, 128)] = pair.astype(BF16)
+
+    loads[0].wait()
+    pack_map(0, sh, 1)
     loads[1].wait()
-    turn(first_t, first)
+    pack_map(1, gsend, 0)
     loads[2].wait()
-    turn(second_t, second)
+    pack_map(2, xsend, 0)
+    loads[3].wait()
+    loads[4].wait()
+
+    @pl.when(sec == nsec - 1)
+    def _():
+        pack_map(3, gh, 1)
+
+    @pl.when(sec == 0)
+    def _():
+        pack_map(4, xh, 1)
 
     pl.semaphore_wait(barrier, len(peers))
 
@@ -112,20 +131,19 @@
         for copy in copies:
             copy.wait()
 
-    saved_halo = halos(saved, sh, sec, 0)
+    saved_halo = halos(sh.at[pl.ds(1, H)], sh, sec, 0)
     start_all(saved_halo)
 
-    def start_map(src, edge_src, local, held, to, k, edge):
+    def start_map(src, held, to, k, edge):
         @pl.when(sec == edge)
         def _():
-            start_all(halos(edge_src, held, sec, k + 3))
-            local.start()
+            start_all(halos(held.at[pl.ds(1, H)], held, sec, k + 3))
 
         @pl.when(sec != nsec - 1 - edge)
         def _():
             start_all(shifted_map(src, held, to, k))
 
-    def wait_map(src, edge_src, local, held, to, k, edge):
+    def wait_map(src, held, to, k, edge):
         copies = shifted_map(src, held, to, k)
 
         @pl.when(sec != nsec - 1 - edge)
@@ -135,40 +153,56 @@
 
         @pl.when(sec == edge)
         def _():
-            edges = halos(edge_src, held, sec, k + 3)
-            for copy in edges:
-                copy.wait_send()
-                copy.wait_recv()
-            local.wait()
+            wait_all(halos(held.at[pl.ds(1, H)], held, sec, k + 3))
 
         @pl.when(sec != edge)
         def _():
             for copy in copies:
                 copy.wait_recv()
 
-    g_map = (sent_grad, loss_grad, local_g, gh, prev_sec, 2, nsec - 1)
-    x_map = (carried, image, local_x, xh, next_sec, 7, 0)
+    g_map = (gsend, gh, prev_sec, 2, nsec - 1)
+    x_map = (xsend, xh, next_sec, 7, 0)
     start_map(*g_map)
+
+    def turn(source, target):
+        for k in range(0, 9 * C, 640):
+            n = min(640, 9 * C - k)
+            target[pl.ds(k, n), :] = jnp.transpose(source[:, pl.ds(k, n)])
+
+    loads[5].wait()
+    turn(first_t, first)
+    loads[6].wait()
+    turn(second_t, second)
 
     terms[pl.ds(9 * C, 8), :] = jnp.zeros((8, CL), F32)
     terms[:, pl.ds(MAIN, CL - MAIN)] = jnp.zeros((9 * C + 8, CL - MAIN), F32)
-    shift_buf[pl.ds(0, 8), :] = jnp.zeros((8, C), F32)
-    shift_buf[pl.ds(8 + 4 * W, 8), :] = jnp.zeros((8, C), F32)
+    shift_buf[pl.ds(0, 8), :] = jnp.zeros((8, CL), F32)
+    shift_buf[pl.ds(8 + 4 * W, 8), :] = jnp.zeros((8, CL), F32)
     column = lax.broadcasted_iota(jnp.int32, (W, C), 0)
 
     def build(held, out):
         for r in range(H + 2):
-            v = held[r]
+            main = held[r, pl.ds(0, W), :]
+            pairs = [held[r, pl.ds(W, Q), pl.ds(128 * j, 128)].astype(F32) for j in range(2)]
+            rest = jnp.concatenate(
+                [part for pair in pairs for part in (pair, pltpu.roll(pair, 64, 1))], axis=0
+            )
+            outside = None
             if r == 0:
-                v = jnp.where(band == 0, jnp.zeros_like(v), v)
+                outside = band == 0
             if r == H + 1:
-                v = jnp.where(band == nband - 1, jnp.zeros_like(v), v)
-            out[1, pl.ds(r * W, W), :] = v
-            shift_buf[pl.ds(8 + r * W, W), :] = v.astype(F32)
+                outside = band == nband - 1
+            if outside is not None:
+                main = jnp.where(outside, jnp.zeros_like(main), main)
+                rest = jnp.where(outside, jnp.zeros_like(rest), rest)
+            rows = pl.ds(8 + r * W, W)
+            shift_buf[rows, pl.ds(0, MAIN)] = main.astype(F32)
+            shift_buf[rows, pl.ds(MAIN, 128)] = rest
+            out[1, pl.ds(r * W, W), :] = shift_buf[rows, pl.ds(0, C)].astype(BF16)
         for r in range(H + 2):
-            low = shift_buf[pl.ds(7 + r * W, W), :]
+            low = shift_buf[pl.ds(7 + r * W, W), pl.ds(0, C)]
             out[0, pl.ds(r * W, W), :] = jnp.where(column == 0, 0.0, low).astype(BF16)
-            high = shift_buf[pl.ds(9 + r * W, W), :]
+            high = shift_buf[pl.ds(9 + r * W, W), pl.ds(0, C)]
             out[2, pl.ds(r * W, W), :] = jnp.where(column == W - 1, 0.0, high).astype(BF16)
 
     def conv(maps, weights):
@@ -281,7 +315,6 @@
     def stage3(k):
         return remote(send3.at[k], recv3.at[k], s3_sem.at[k], r3_sem.at[k], z_peer)
 
-    loads[0].wait()
     wait_all(saved_halo)
     build(sh, ss)
     pre = conv(ss, first)
@@ -298,7 +331,8 @@
 
     grad_pre = (conv_t(gs, second) * slope[...]).astype(BF16)
     for r in range(H):
-        ph[1 + r] = grad_pre[r * W : (r + 1) * W]
+        raw[0, r] = grad_pre[r * W : (r + 1) * W]
+    pack_map(0, ph, 1)
     pre_halo = halos(ph.at[pl.ds(1, H)], ph, sec, 12)
     start_all(pre_halo)
 
@@ -314,36 +348,37 @@
     first_relays, first_plain, first_added = stage1(0)
     start_all(first_relays + first_plain)
 
+    wait_all(first_relays)
+    add_relays(0)
+    start_all(first_added)
+
+    wait_all(second_plain + second_added)
+    sum1(1)
+    second_2 = stage2(1)
+    start_all(second_2)
+
     wait_map(*x_map)
     build(xh, xs)
     pre = conv(xs, first)
     act = (pre * jax.nn.sigmoid(pre)).astype(BF16)
     for r in range(H):
-        ah[1 + r] = act[r * W : (r + 1) * W]
+        raw[1, r] = act[r * W : (r + 1) * W]
+    pack_map(1, ah, 1)
     act_halo = halos(ah.at[pl.ds(1, H)], ah, sec, 14)
     start_all(act_halo)
 
-    wait_all(first_relays)
-    add_relays(0)
-    start_all(first_added)
-
-    wait_all(second_plain + second_added)
-    sum1(1)
-    second_2 = stage2(1)
-    start_all(second_2)
+    wait_all(first_plain + first_added)
+    sum1(0)
+    first_2 = stage2(0)
+    start_all(first_2)
 
     wait_all(pre_halo)
     build(ph, ps)
     igrad_flat = conv_t(ps, first)
     for r in range(H):
-        igrad[r] = (gh[1 + r].astype(F32) + igrad_flat[r * W : (r + 1) * W]).astype(BF16)
+        igrad[r] = (gs[1, pl.ds((1 + r) * W, W), :].astype(F32) + igrad_flat[r * W : (r + 1) * W]).astype(BF16)
     outs = [pltpu.make_async_copy(igrad, igrad_hbm, out_sem.at[0])]
     outs[0].start()
-
-    wait_all(first_plain + first_added)
-    sum1(0)
-    first_2 = stage2(0)
-    start_all(first_2)
 
     wait_all(second_2)
     sum2(1)
@@ -359,7 +394,7 @@
     build(ah, as_)
     out_flat = conv(as_, second)
     for r in range(H):
-        fwd[r] = (xh[1 + r].astype(F32) + out_flat[r * W : (r + 1) * W]).astype(BF16)
+        fwd[r] = (xs[1, pl.ds((1 + r) * W, W), :].astype(F32) + out_flat[r * W : (r + 1) * W]).astype(BF16)
     outs.append(pltpu.make_async_copy(fwd, fwd_hbm, out_sem.at[1]))
     outs[1].start()
 
@@ -383,7 +418,7 @@
     factor = 1.0 / math.sqrt(H * lax.axis_size("band") * W)
     any_spec = pl.BlockSpec(memory_space=pl.ANY)
     vmem, dma = pltpu.VMEM, pltpu.SemaphoreType.DMA
-    halo_map = vmem((H + 2, W, C), BF16)
+    halo_map = vmem((H + 2, ROW, MAIN), BF16)
     moved = vmem((3, (H + 2) * W, C), BF16)
     fwd, igrad, gfirst, gsecond = pl.pallas_call(
         functools.partial(kernel, factor),
@@ -398,9 +433,10 @@
         scratch_shapes=[
             vmem((C, 9 * C), BF16), vmem((C, 9 * C), BF16),
             vmem((9 * C, C), BF16), vmem((9 * C, C), BF16),
+            vmem((5, H, W, C), BF16), vmem((H, ROW, MAIN), BF16), vmem((H, ROW, MAIN), BF16),
             halo_map, halo_map, halo_map, halo_map, halo_map,
             moved, moved, moved, moved, moved,
-            vmem((16 + (H + 2) * W, C), F32),
+            vmem((16 + (H + 2) * W, CL), F32),
             vmem((M, C), F32),
             vmem((C, M), BF16),
             vmem((9 * C + 8, CL), F32),
@@ -411,7 +447,7 @@
             vmem((2, PR, CL), BF16), vmem((2, PR, CL), BF16), vmem((2, PR, CL), F32),
             vmem((H, W, C), BF16), vmem((H, W, C), BF16),
             vmem((2, PIECE, C), F32),
-            dma((5,)), dma((16,)), dma((16,)),
+            dma((7,)), dma((16,)), dma((16,)),
             dma((2, 2, 6)), dma((2, 2, 6)), dma((2, 2, 3)), dma((2, 2, 3)),
             dma((2,)), dma((2,)), dma((4,)),
         ],

time: 72.3 us -> 68.7 us (0.950)
  Pallas kernels: 71.5 us -> 67.6 us
    pallas_call x1, Pallas kernels: 69.4 us -> 65.4 us  [body(): pl.pallas_call(functools.partial(kernel, factor), out_shape=(jax.ShapeDty...]
where the time goes in v2:
time: 68.7 us; the launch traced here: 68.2 us
  Pallas kernels  67.6 us (98%)
    pallas_call x1, Pallas kernels, body(): pl.pallas_call(functools.partial(kernel, factor), out_shape=(jax.ShapeDty...  65.4 us
    pallas_call x1, Pallas kernels, body(): pl.pallas_call(copy_out, out_shape=(fwd, igrad, grad_shape, grad_shape),...  2.12 us

profile of v2, /device:TPU:6, one launch (start us, length us, event | category | flops | bytes accessed | tf_op | source)
XLA Modules:
  0.0 68.2 jit_solution(2000550610588312975)
XLA Ops:
  0.6 65.4 %shard_map.102 = (bf16[2,160,320]{2,1,0:T(8,128)(2,1)}, bf16[2,160,320]{2,1,0:T(8,128)(2,1)}, f32[90,320]{1,0:T(8,128)}, f32[90,320]{1,0:T(8,128)}) custom-call(bf16[2,160,320]{2,1,0:T(8,128)(2,1)} %image.1, bf16[2,160,320]{2,1,0:T(8,128)(2,1)} %bitcast.15, bf16[2,160,320]{2,1,0:T(8,128)(2,1)} %bitcast.16, bf16[2,160,320]{2,1,0:T(8,128)(2,1)} %bitcast.17, ...), custom_call_target="tpu_custom_call" | custom-call | tf_op jit(solution)/shard_map/pallas_call | solution.py:423
  66.1 2.1 %shard_map.103 = (bf16[2,160,320]{2,1,0:T(8,128)(2,1)}, bf16[2,160,320]{2,1,0:T(8,128)(2,1)}, f32[90,1,320]{2,1,0:T(1,128)}, f32[90,1,320]{2,1,0:T(1,128)}) custom-call(bf16[2,160,320]{2,1,0:T(8,128)(2,1)} %get-tuple-element.12.fwd, bf16[2,160,320]{2,1,0:T(8,128)(2,1)} %get-tuple-element.13.igrad, f32[90,320]{1,0:T(8,128)} %get-tuple-element.14.gfirst, ...), custom_call_target="tpu_custom_call" | custom-call | tf_op jit(solution)/shard_map/pallas_call | solution.py:460

commit v3 on v2

--- a/solution.py
+++ b/solution.py
@@ -34,10 +34,10 @@
 
 def kernel(
     factor, image, carried, saved, sent_grad, loss_grad, first_hbm, second_hbm,
-    fwd_hbm, igrad_hbm, gfirst_hbm, gsecond_hbm,
+    fwd, igrad, gfirst, gsecond,
     first_t, second_t, first, second, raw, gsend, xsend, xh, sh, gh, ah, ph, xs, ss, gs, as_, ps, shift_buf, slope, actt,
-    terms, send1, relay, recv1, held2, send2, recv2, send3, recv3, keep3, fwd, igrad, gout,
-    load_sem, halo_send, halo_recv, s1_sem, r1_sem, s2_sem, r2_sem, s3_sem, r3_sem, out_sem,
+    terms, send1, relay, recv1, held2, send2, recv2, send3, recv3, keep3,
+    load_sem, halo_send, halo_recv, s1_sem, r1_sem, s2_sem, r2_sem, s3_sem, r3_sem,
 ):
     sec = lax.axis_index("section")
     band = lax.axis_index("band")
@@ -377,8 +377,6 @@
     igrad_flat = conv_t(ps, first)
     for r in range(H):
         igrad[r] = (gs[1, pl.ds((1 + r) * W, W), :].astype(F32) + igrad_flat[r * W : (r + 1) * W]).astype(BF16)
-    outs = [pltpu.make_async_copy(igrad, igrad_hbm, out_sem.at[0])]
-    outs[0].start()
 
     wait_all(second_2)
     sum2(1)
@@ -395,16 +393,10 @@
     out_flat = conv(as_, second)
     for r in range(H):
         fwd[r] = (xs[1, pl.ds((1 + r) * W, W), :].astype(F32) + out_flat[r * W : (r + 1) * W]).astype(BF16)
-    outs.append(pltpu.make_async_copy(fwd, fwd_hbm, out_sem.at[1]))
-    outs[1].start()
-
-    for k, copy, out in ((1, second_3, gsecond_hbm), (0, first_3, gfirst_hbm)):
+
+    for k, copy, out in ((1, second_3, gsecond), (0, first_3, gfirst)):
         copy.wait()
-        gout[k] = (keep3[k] + recv3[k].astype(F32))[:PIECE, :C] * factor
-        outs.append(pltpu.make_async_copy(gout.at[k], out, out_sem.at[3 - k]))
-        outs[-1].start()
-    for copy in outs:
-        copy.wait()
+        out[...] = (keep3[k] + recv3[k].astype(F32))[:PIECE, :C] * factor
 
 
 def copy_out(fwd, igrad, gfirst, gsecond, fwd_out, igrad_out, gfirst_out, gsecond_out):
@@ -417,19 +409,17 @@
 def body(image, carried, saved, sent_grad, loss_grad, first_kernel, second_kernel):
     factor = 1.0 / math.sqrt(H * lax.axis_size("band") * W)
     any_spec = pl.BlockSpec(memory_space=pl.ANY)
+    vmem_spec = pl.BlockSpec(memory_space=pltpu.VMEM)
     vmem, dma = pltpu.VMEM, pltpu.SemaphoreType.DMA
     halo_map = vmem((H + 2, ROW, MAIN), BF16)
     moved = vmem((3, (H + 2) * W, C), BF16)
     fwd, igrad, gfirst, gsecond = pl.pallas_call(
         functools.partial(kernel, factor),
         out_shape=(
-            jax.ShapeDtypeStruct((H, W, C), BF16),
-            jax.ShapeDtypeStruct((H, W, C), BF16),
-            jax.ShapeDtypeStruct((PIECE, C), F32),
-            jax.ShapeDtypeStruct((PIECE, C), F32),
+            vmem((H, W, C), BF16), vmem((H, W, C), BF16), vmem((PIECE, C), F32), vmem((PIECE, C), F32),
         ),
         in_specs=[any_spec] * 7,
-        out_specs=(any_spec,) * 4,
+        out_specs=(vmem_spec,) * 4,
         scratch_shapes=[
             vmem((C, 9 * C), BF16), vmem((C, 9 * C), BF16),
             vmem((9 * C, C), BF16), vmem((9 * C, C), BF16),
@@ -445,24 +435,22 @@
             vmem((2, 2, 4, PR, CL), F32), vmem((2, 2, 4, PR, CL), BF16),
             vmem((2, 2, 3, PR, CL), BF16),
             vmem((2, PR, CL), BF16), vmem((2, PR, CL), BF16), vmem((2, PR, CL), F32),
-            vmem((H, W, C), BF16), vmem((H, W, C), BF16),
-            vmem((2, PIECE, C), F32),
             dma((7,)), dma((16,)), dma((16,)),
             dma((2, 2, 6)), dma((2, 2, 6)), dma((2, 2, 3)), dma((2, 2, 3)),
-            dma((2,)), dma((2,)), dma((4,)),
+            dma((2,)), dma((2,)),
         ],
         compiler_params=pltpu.CompilerParams(
             collective_id=0, has_side_effects=True, vmem_limit_bytes=56 * 1024 * 1024
         ),
     )(image, carried[0], saved[0], sent_grad[0], loss_grad, first_kernel[0].T, second_kernel[0].T)
-    vmem_spec = pl.BlockSpec(memory_space=pltpu.VMEM)
+    map_shape = jax.ShapeDtypeStruct((H, W, C), BF16)
     grad_shape = jax.ShapeDtypeStruct((PIECE, 1, C), F32)
     fwd, igrad, gfirst, gsecond = pl.pallas_call(
         copy_out,
-        out_shape=(fwd, igrad, grad_shape, grad_shape),
+        out_shape=(map_shape, map_shape, grad_shape, grad_shape),
         in_specs=[vmem_spec] * 4,
         out_specs=(vmem_spec,) * 4,
-    )(fwd, igrad, gfirst, gsecond)
+    )(*[pltpu.with_memory_space_constraint(v, pltpu.VMEM) for v in (fwd, igrad, gfirst, gsecond)])
     return fwd[None], igrad[None], gfirst.reshape(1, PIECE, C), gsecond.reshape(1, PIECE, C)
 
 

time: 68.7 us -> 66.8 us (0.972)
  Pallas kernels: 67.6 us -> 65.7 us
    pallas_call x2, Pallas kernels: 67.6 us -> 65.7 us  [the longest x1 64.7 us: body(): pl.pallas_call(functools.partial(kernel, factor), out_shape=(vmem((H, W,...]
where the time goes in v3:
time: 66.8 us; the launch traced here: 66.3 us
  Pallas kernels  65.7 us (98%)
    pallas_call x1, Pallas kernels, body(): pl.pallas_call(functools.partial(kernel, factor), out_shape=(vmem((H, W,...  64.7 us

profile of v3, /device:TPU:6, one launch (start us, length us, event | category | flops | bytes accessed | tf_op | source)
XLA Modules:
  0.0 66.3 jit_solution(9145659654939955639)
XLA Ops:
  0.6 64.7 %shard_map.102 = (bf16[2,160,320]{2,1,0:T(8,128)(2,1)S(1)}, bf16[2,160,320]{2,1,0:T(8,128)(2,1)S(1)}, f32[90,320]{1,0:T(8,128)S(1)}, f32[90,320]{1,0:T(8,128)S(1)}) custom-call(bf16[2,160,320]{2,1,0:T(8,128)(2,1)} %image.1, bf16[2,160,320]{2,1,0:T(8,128)(2,1)} %bitcast.15, bf16[2,160,320]{2,1,0:T(8,128)(2,1)} %bitcast.16, bf16[2,160,320]{2,1,0:T(8,128)(2,1)} %bitcast.17, ...), custom_call_target="tpu_custom_call" | custom-call | tf_op jit(solution)/shard_map/pallas_call | solution.py:416
  65.4 0.9 %shard_map.103 = (bf16[2,160,320]{2,1,0:T(8,128)(2,1)}, bf16[2,160,320]{2,1,0:T(8,128)(2,1)}, f32[90,1,320]{2,1,0:T(1,128)}, f32[90,1,320]{2,1,0:T(1,128)}) custom-call(bf16[2,160,320]{2,1,0:T(8,128)(2,1)S(1)} %get-tuple-element.12.fwd, bf16[2,160,320]{2,1,0:T(8,128)(2,1)S(1)} %get-tuple-element.13.igrad, f32[90,320]{1,0:T(8,128)S(1)} %get-tuple-element.14.gfirst, ...), custom_call_target="tpu_custom_call" | custom-call | tf_op jit(solution)/shard_map/pallas_call | solution.py:448

commit v4 on v3

--- a/solution.py
+++ b/solution.py
@@ -19,6 +19,7 @@
 PR = 96
 MAIN = 256
 SEND = 5 * PR
+PQ = PR // 4
 Q = W // 4
 ROW = W + Q
 NX, NY, NZ = 4, 4, 2
@@ -91,18 +92,11 @@
     pack_map(0, sh, 1)
     loads[1].wait()
     pack_map(1, gsend, 0)
-    loads[2].wait()
-    pack_map(2, xsend, 0)
     loads[3].wait()
-    loads[4].wait()
 
     @pl.when(sec == nsec - 1)
     def _():
         pack_map(3, gh, 1)
-
-    @pl.when(sec == 0)
-    def _():
-        pack_map(4, xh, 1)
 
     pl.semaphore_wait(barrier, len(peers))
 
@@ -163,6 +157,14 @@
     g_map = (gsend, gh, prev_sec, 2, nsec - 1)
     x_map = (xsend, xh, next_sec, 7, 0)
     start_map(*g_map)
+
+    loads[2].wait()
+    pack_map(2, xsend, 0)
+    loads[4].wait()
+
+    @pl.when(sec == 0)
+    def _():
+        pack_map(4, xh, 1)
 
     def turn(source, target):
         for k in range(0, 9 * C, 640):
@@ -295,20 +297,31 @@
             for j in range(4):
                 main = total(pl.ds(j * PR, PR), pl.ds(0, MAIN))
                 held2[k, half, j, :, pl.ds(0, MAIN)] = main
-                send2[k, half, j, :, pl.ds(0, MAIN)] = main.astype(BF16)
+                send2[k, half, j, pl.ds(0, PR), :] = main.astype(BF16)
             for j in range(2):
                 rest = total(pl.ds(4 * PR, PR), pl.ds(j * 128, 128))
                 for i, part in enumerate((rest, pltpu.roll(rest, 64, 1))):
                     held2[k, half, 2 * j + i, :, pl.ds(MAIN, 128)] = part
-                    send2[k, half, 2 * j + i, :, pl.ds(MAIN, 128)] = part.astype(BF16)
+                    for p in range(2):
+                        one, two = part[2 * p * PQ : (2 * p + 1) * PQ], part[(2 * p + 1) * PQ : (2 * p + 2) * PQ]
+                        pair = jnp.where(lane[:PQ] < 64, one, pltpu.roll(two, 64, 1))
+                        send2[k, half, 2 * j + i, pl.ds(PR, PQ), pl.ds(128 * p, 128)] = pair.astype(BF16)
 
     def sum2(k):
         sums = []
         for half, pos in enumerate((y, x)):
-            value = held2[k, half, pos]
+            main, rest = held2[k, half, pos, :, pl.ds(0, MAIN)], held2[k, half, pos, :, pl.ds(MAIN, 128)]
+            pairs = []
+            for p in range(2):
+                pairs.append(jnp.zeros((PQ, 128), F32))
+                for d in range(3):
+                    pairs[p] = pairs[p] + recv2[k, half, d, pl.ds(PR, PQ), pl.ds(128 * p, 128)].astype(F32)
             for d in range(3):
-                value = value + recv2[k, half, d].astype(F32)
-            sums.append(value)
+                main = main + recv2[k, half, d, pl.ds(0, PR), :].astype(F32)
+            rest = rest + jnp.concatenate(
+                [part for pair in pairs for part in (pair, pltpu.roll(pair, 64, 1))], axis=0
+            )
+            sums.append(jnp.concatenate([main, rest], axis=1))
         keep3[k] = jnp.where(z == 0, sums[0], sums[1])
         send3[k] = jnp.where(z == 0, sums[1], sums[0]).astype(BF16)
 
@@ -372,16 +385,16 @@
     first_2 = stage2(0)
     start_all(first_2)
 
+    wait_all(second_2)
+    sum2(1)
+    second_3 = stage3(1)
+    second_3.start()
+
     wait_all(pre_halo)
     build(ph, ps)
     igrad_flat = conv_t(ps, first)
     for r in range(H):
         igrad[r] = (gs[1, pl.ds((1 + r) * W, W), :].astype(F32) + igrad_flat[r * W : (r + 1) * W]).astype(BF16)
-
-    wait_all(second_2)
-    sum2(1)
-    second_3 = stage3(1)
-    second_3.start()
 
     wait_all(first_2)
     sum2(0)
@@ -432,8 +445,8 @@
             vmem((9 * C + 8, CL), F32),
             vmem((2, 2, 4, SEND, MAIN), BF16), vmem((2, 2, 2, SEND // 2, MAIN), BF16),
             vmem((2, 2, 2, SEND, MAIN), BF16),
-            vmem((2, 2, 4, PR, CL), F32), vmem((2, 2, 4, PR, CL), BF16),
-            vmem((2, 2, 3, PR, CL), BF16),
+            vmem((2, 2, 4, PR, CL), F32), vmem((2, 2, 4, PR + PQ, MAIN), BF16),
+            vmem((2, 2, 3, PR + PQ, MAIN), BF16),
             vmem((2, PR, CL), BF16), vmem((2, PR, CL), BF16), vmem((2, PR, CL), F32),
             dma((7,)), dma((16,)), dma((16,)),
             dma((2, 2, 6)), dma((2, 2, 6)), dma((2, 2, 3)), dma((2, 2, 3)),

time: 66.8 us -> 66 us (0.988)
  no operation moved by 1% of the time
where the time goes in v4:
time: 66 us
  Pallas kernels  65.3 us (99%)
    pallas_call x1, Pallas kernels, body(): pl.pallas_call(functools.partial(kernel, factor), out_shape=(vmem((H, W,...  64.4 us

profile of v4, /device:TPU:6, one launch (start us, length us, event | category | flops | bytes accessed | tf_op | source)
XLA Modules:
  0.0 66.0 jit_solution(764124478568190378)
XLA Ops:
  0.6 64.4 %shard_map.102 = (bf16[2,160,320]{2,1,0:T(8,128)(2,1)S(1)}, bf16[2,160,320]{2,1,0:T(8,128)(2,1)S(1)}, f32[90,320]{1,0:T(8,128)S(1)}, f32[90,320]{1,0:T(8,128)S(1)}) custom-call(bf16[2,160,320]{2,1,0:T(8,128)(2,1)} %image.1, bf16[2,160,320]{2,1,0:T(8,128)(2,1)} %bitcast.15, bf16[2,160,320]{2,1,0:T(8,128)(2,1)} %bitcast.16, bf16[2,160,320]{2,1,0:T(8,128)(2,1)} %bitcast.17, ...), custom_call_target="tpu_custom_call" | custom-call | tf_op jit(solution)/shard_map/pallas_call | solution.py:429
  65.0 0.9 %shard_map.103 = (bf16[2,160,320]{2,1,0:T(8,128)(2,1)}, bf16[2,160,320]{2,1,0:T(8,128)(2,1)}, f32[90,1,320]{2,1,0:T(1,128)}, f32[90,1,320]{2,1,0:T(1,128)}) custom-call(bf16[2,160,320]{2,1,0:T(8,128)(2,1)S(1)} %get-tuple-element.12.fwd, bf16[2,160,320]{2,1,0:T(8,128)(2,1)S(1)} %get-tuple-element.13.igrad, f32[90,320]{1,0:T(8,128)S(1)} %get-tuple-element.14.gfirst, ...), custom_call_target="tpu_custom_call" | custom-call | tf_op jit(solution)/shard_map/pallas_call | solution.py:461
